TPU v7x, 32 devices: a whole 2x2x4 slice. The times are simulated.
32 devices in a mesh: seq: 16 (over z, x, core), head: 2 (over y).
Axes of the slice: x: 2, y: 2, z: 4, core: 2. Of those that a mesh axis runs over, the one named last changes fastest.
Arguments:
- queries: bfloat16 [12288, 4096], P('seq', 'head'), may hold values from -100 to 100
- keys: bfloat16 [12288, 4096], P('seq', 'head'), may hold values from -7 to 7
- values: bfloat16 [12288, 4096], P('seq', 'head'), may hold values from -6 to 6
- targets: bfloat16 [12288, 4096], P('seq', 'head'), may hold values from -6 to 6
- token_rate: float32 [12288, 8], P('seq', 'head'), may hold values from 0.1 to 1
- window: int32 [8], P('head'), may hold values from 256 to 512, as said below
- split: int32 [1], replicated, may hold values from 4608 to 7679
- fast_init: float32 [8, 3, 512, 512], P('head'), may hold values from -0.25 to 0.25
Outputs:
- mixed: bfloat16 [12288, 4096], P('seq', 'head')
- fast_final: float32 [8, 3, 512, 512], P('head')
Inputs may be any that keep to these rules, and one draw needn't show every extreme that they name: Some head has a window of exactly 512.
All inputs are finite; a program needn't handle non-finite values.
Results may differ from a plain program's by a relative error of at most 0.0073.
Values may be sent and summed in bfloat16 or wider, within the bound.
A program may use at most 192 MiB of HBM per device.

v0:
```python
import functools

import jax
import jax.numpy as jnp
from jax import lax
from jax.experimental import pallas as pl
from jax.experimental.pallas import tpu as pltpu
from jax.sharding import PartitionSpec as P

WIN = 512
fast_rate = 0.01
epsilon = 1e-06
CORES = 2


def mm(a, b, ca, cb):
    return lax.dot_general(
        a, b, (((ca,), (cb,)), ((), ())), preferred_element_type=jnp.float32
    )


SHARES = (8, 4, 4)
STEPS = (1, 2, 2)
CHUNK = 256


class Link:
    def __init__(self, net, src, dst, to, gives):
        self.net, self.src, self.dst, self.to, self.gives = net, src, dst, to, gives
        self.kind = len(net.links)
        net.links.append(self)

    def copy(self, n, slot):
        return pltpu.make_async_remote_copy(
            src_ref=self.src(n),
            dst_ref=self.dst(n),
            send_sem=self.net.send.at[self.kind],
            recv_sem=self.net.recv.at[self.kind, slot],
            device_id={"seq": self.to},
            device_id_type=pl.DeviceIdType.MESH,
        )

    def start(self, n):
        @pl.when(self.gives)
        def _():
            self.copy(n, n).start()

    def wait(self, n):
        self.copy(n, n).wait_recv()

    def drain(self):
        @pl.when(self.gives)
        def _():
            self.copy(pl.ds(0, self.net.chunks), 0).wait_send()


def total(ref, at, parts):
    out = ref[at].astype(jnp.float32)
    for part in parts:
        out += part.astype(jnp.float32)
    return out.astype(ref.dtype)


def link_kinds(near):
    return 2 + (4 + 2 * (near - 1)) + 2 * (4 + 2 * (near - 1))


class Net:
    def __init__(self, mirror, near_size, far_size, g, out, acc, got, send, recv):
        self.links, self.stages = [], []
        self.send, self.recv = send, recv
        self.chunks, rows, width = g.shape
        half = rows // CORES
        fine = width // near_size
        me = lax.axis_index("seq")
        core = me % CORES
        near = (me // CORES) % near_size
        far = me // (CORES * near_size)
        line = far_size - 1 - far if mirror else far
        last = (5 * far_size - 1) // 8
        gives = line <= last
        step_core, step_near, step_line = STEPS

        def device(line_to, near_to, core_to):
            far_to = far_size - 1 - line_to if mirror else line_to
            return (far_to * near_size + near_to) * CORES + core_to

        def peer(d):
            return device(line, (near + d) % near_size, core)

        def piece(d):
            index = (near + d) % near_size
            return pl.ds(pl.multiple_of(index * fine, 128), fine)

        def rows_of(c, first, count):
            return pl.ds(pl.multiple_of(c * half + first, 16), count)

        other = 1 - core
        mate = device(line, near, other)
        swap = Link(self, lambda n: g.at[n, rows_of(other, 0, half)], lambda n: acc.at[n], mate, gives)
        join = Link(
            self,
            lambda n: out.at[n, rows_of(core, 0, half)],
            lambda n: out.at[n, rows_of(core, 0, half)],
            mate,
            me >= 0,
        )
        self.stage(0, swap.start)

        unit = half // sum(SHARES)
        count = [s * unit for s in SHARES]
        first = [sum(count[:i]) for i in range(3)]
        mid = last // 2
        ends = []
        starts = []

        def line_links(root, src, base, n_cols, final):
            left = Link(self, src, lambda n: got.at[0, n, base, n_cols], device(line + 1, near, core), line < root)
            right = Link(
                self, src, lambda n: got.at[1, n, base, n_cols], device(line - 1, near, core),
                (line > root) & gives,
            )
            out_right = Link(self, final, final, device(line + 1, near, core), (line >= root) & (line < far_size - 1))
            out_left = Link(self, final, final, device(line - 1, near, core), (line <= root) & (line > 0))
            return left, right, out_right, out_left

        def line_in(at, root, left, right, base, cols, done):
            depth = max(root, last - root)

            def begin(n):
                @pl.when(line == 0)
                def _():
                    left.start(n)

                @pl.when(line == last)
                def _():
                    right.start(n)

            def hop(k, n):
                if k < root:
                    @pl.when(line == k)
                    def _():
                        left.wait(n)
                        acc[n, base, cols] = total(acc, (n, base, cols), [got[0, n, base, cols]])
                        left.start(n)
                if last - k > root:
                    @pl.when(line == last - k)
                    def _():
                        right.wait(n)
                        acc[n, base, cols] = total(acc, (n, base, cols), [got[1, n, base, cols]])
                        right.start(n)

            def end(n):
                @pl.when(line == root)
                def _():
                    parts = []
                    if root > 0:
                        left.wait(n)
                        parts.append(got[0, n, base, cols])
                    if last > root:
                        right.wait(n)
                        parts.append(got[1, n, base, cols])
                    done(n, total(acc, (n, base, cols), parts))

            for k in range(1, depth):
                self.stage(at + k * step_line, functools.partial(hop, k))
            self.stage(at + depth * step_line, end)
            return begin, at + depth * step_line

        def line_out(at, root, out_right, out_left, then):
            def hop(k, n):
                if root + k < far_size:
                    @pl.when(line == root + k)
                    def _():
                        out_right.wait(n)
                        out_right.start(n)
                        then(n)
                if root - k >= 0:
                    @pl.when(line == root - k)
                    def _():
                        out_left.wait(n)
                        out_left.start(n)
                        then(n)

            depth = max(far_size - 1 - root, root)
            for k in range(1, depth + 1):
                self.stage(at + k * step_line, functools.partial(hop, k))
            return at + depth * step_line

        t = step_core

        if count[0]:
            base = pl.ds(first[0], count[0])
            wide = rows_of(core, first[0], count[0])
            mine = piece(0)
            spread = [
                Link(
                    self,
                    lambda n, d=d: acc.at[n, base, piece(d)],
                    lambda n, d=d: got.at[2, n, base, pl.ds((d - 1) * fine, fine)],
                    peer(d),
                    gives,
                )
                for d in range(1, near_size)
            ]
            final = lambda n: out.at[n, wide, mine]
            left, right, out_right, out_left = line_links(mid, lambda n: acc.at[n, base, mine], base, mine, final)
            fill = [Link(self, final, final, peer(d), me >= 0) for d in range(1, near_size)]
            starts += spread

            def give(n):
                for f in fill:
                    f.start(n)

            def done(n, value):
                out[n, wide, mine] = value
                out_right.start(n)
                out_left.start(n)
                give(n)

            begin, t1 = line_in(t + step_near, mid, left, right, base, mine, done)

            def gathered(n):
                @pl.when(gives)
                def _():
                    for s in spread:
                        s.wait(n)
                    acc[n, base, mine] = total(
                        acc, (n, base, mine),
                        [got[2, n, base, pl.ds((d - 1) * fine, fine)] for d in range(1, near_size)],
                    )
                    begin(n)

            self.stage(t + step_near, gathered)
            t1 = line_out(t1, mid, out_right, out_left, give) + step_near

            def filled(n):
                for d in range(1, near_size):
                    fill[d - 1].wait(n)

            self.stage(t1, filled)
            ends.append(t1)

        def whole(index, root):
            base = pl.ds(first[index], count[index])
            wide = rows_of(core, first[index], count[index])
            every = pl.ds(0, width)
            mine = piece(0)
            final = lambda n: out.at[n, wide, every]
            part = lambda n: out.at[n, wide, mine]
            left, right, out_right, out_left = line_links(root, lambda n: acc.at[n, base, every], base, every, final)
            spread = [
                Link(
                    self,
                    lambda n, d=d: acc.at[n, base, piece(d)],
                    lambda n, d=d: got.at[2, n, base, pl.ds((d - 1) * fine, fine)],
                    peer(d),
                    line == root,
                )
                for d in range(1, near_size)
            ]
            fill = [Link(self, part, part, peer(d), line == root) for d in range(1, near_size)]

            def done(n, value):
                acc[n, base, every] = value
                for s in spread:
                    s.start(n)

            begin, t1 = line_in(t, root, left, right, base, every, done)

            def gathered(n):
                @pl.when(line == root)
                def _():
                    for s in spread:
                        s.wait(n)
                    out[n, wide, mine] = total(
                        acc, (n, base, mine),
                        [got[2, n, base, pl.ds((d - 1) * fine, fine)] for d in range(1, near_size)],
                    )
                    for f in fill:
                        f.start(n)

            def filled(n):
                @pl.when(line == root)
                def _():
                    for f in fill:
                        f.wait(n)
                    out_right.start(n)
                    out_left.start(n)

            self.stage(t1 + step_near, gathered)
            self.stage(t1 + 2 * step_near, filled)
            t1 = line_out(t1 + 2 * step_near, root, out_right, out_left, lambda n: None)
            ends.append(t1)
            return begin

        begins = [whole(i, root) for i, root in ((1, mid), (2, last)) if count[i]]

        def paired(n):
            @pl.when(gives)
            def _():
                swap.wait(n)
                acc[n] = total(acc, (n,), [g[n, rows_of(core, 0, half)]])
                for s in starts:
                    s.start(n)
                for begin in begins:
                    begin(n)

        self.stage(t, paired)
        t = max(ends)
        self.stage(t, join.start)
        self.stage(t + step_core, join.wait)
        self.length = self.chunks + t + step_core

    def stage(self, at, fn):
        self.stages.append((at, fn))

    def advance(self, i, finish):
        end = max(at for at, _ in self.stages)
        for at, fn in sorted(self.stages, key=lambda s: -s[0]):
            n = i - at

            @pl.when((n >= 0) & (n < self.chunks))
            def _():
                fn(n)
                if at == end:
                    finish(n)

    def drain(self):
        for link in self.links:
            link.drain()


BLOCK = 256
HALO_EVERY = 5


def sizes_of_seq():
    chips = lax.axis_size("seq") // CORES
    near = 1
    while near * near * 4 <= chips:
        near *= 2
    return near, chips // near


def greet(near_size, far_size):
    me = lax.axis_index("seq")
    strides = (1, CORES, CORES * near_size)
    sizes = (CORES, near_size, far_size)
    all_count = CORES * near_size * far_size
    barrier = pltpu.get_barrier_semaphore()
    targets = [{"seq": (me + d) % all_count} for d in (1, all_count - 1)]
    for stride, size in zip(strides, sizes):
        place = (me // stride) % size
        for d in range(1, size):
            targets.append({"seq": me + ((place + d) % size - place) * stride})
    mine = lax.axis_index("head")
    heads = lax.axis_size("head")
    for d in range(1, heads):
        targets.append({"head": (mine + d) % heads})
    for target in targets:
        pl.semaphore_signal(barrier, inc=1, device_id=target, device_id_type=pl.DeviceIdType.MESH)
    pl.semaphore_wait(barrier, len(targets))


def fast_output(x, wb, head):
    first = mm(x, wb[head, 0], 1, 0)
    third = mm(x, wb[head, 1], 1, 0)
    act = (first * jax.nn.sigmoid(first) * third).astype(jnp.bfloat16)
    y = mm(act, wb[head, 2], 1, 1)
    return y / jnp.sqrt(jnp.mean(y * y, axis=1, keepdims=True) + epsilon)


def share_squares(sq_all, sq_ref, sq_send, sq_recv):
    mine = lax.axis_index("head")
    heads = lax.axis_size("head")
    copies = []
    for d in range(1, heads):
        copies.append(
            pltpu.make_async_remote_copy(
                src_ref=sq_all.at[mine],
                dst_ref=sq_all.at[mine],
                send_sem=sq_send.at[d],
                recv_sem=sq_recv.at[d],
                device_id={"head": (mine + d) % heads},
                device_id_type=pl.DeviceIdType.MESH,
            )
        )
    for c in copies:
        c.start()
    for c in copies:
        c.wait()
    sq_ref[...] = jnp.sum(sq_all[...], axis=0)


def block_kernel(second, near_size, far_size, total_count, *refs):
    refs = list(refs)

    def take(count):
        out = refs[:count]
        del refs[:count]
        return out

    if second:
        edge_ref, rate_ref, sq_in, keys, queries, targets, weights, g_in, attn = take(9)
        sums, sq_ref, mixed = take(3)
    else:
        edge_ref, win_ref, rate_ref, keys, values, queries, targets, weights = take(8)
        sums, sq_ref, attn = take(3)
    kbuf, qbuf, tbuf, wbuf, wb, g, res, acc, got, dbuf, stage, sq_all = take(12)
    send, recv, sq_send, sq_recv, load, wload, out_sem, stage_sem = take(8)
    if second:
        gbuf, mstage, in_sem = take(3)
        pad = 0
    else:
        vbuf, halo_send, halo_recv = take(3)
        pad = WIN
    assert not refs

    heads = weights.shape[0]
    local, hd = qbuf.shape[1:]
    me = lax.axis_index("seq")
    count = lax.axis_size("seq")
    mine = lax.axis_index("head")
    anchor = me * local
    early = 8 * me < 5 * count
    late = 8 * (me + 1) > 3 * count
    works = late if second else early
    far = me // (CORES * near_size)
    line = far_size - 1 - far if second else far
    gives = line <= (5 * far_size - 1) // 8
    pieces = hd // CHUNK
    per = 3 * pieces
    blocks = local // BLOCK
    units = blocks * heads
    begin = (heads - 1) * (per - 1)
    edge = edge_ref[0]

    def columns(ref, h, rows=None):
        cols = pl.ds(pl.multiple_of(h * hd, 128), hd)
        return ref.at[pl.ds(0, local) if rows is None else rows, cols]

    def load_weights(h):
        copies = [pltpu.make_async_copy(weights.at[h], wbuf, wload.at[0])]
        if second:
            copies.append(
                pltpu.make_async_copy(g_in.at[pl.ds(pl.multiple_of(h * per, per), per)], gbuf, wload.at[1])
            )
        return copies

    def load_one(i, h):
        src = (keys, targets, queries, None if second else values)[i]
        dst = (kbuf, tbuf, qbuf, None if second else vbuf)[i]
        at = dst.at[h, pl.ds(pad, local)] if i in (0, 3) else dst.at[h]
        return pltpu.make_async_copy(columns(src, h), at, load.at[i, h])

    def place(u):
        return blocks - 1 - u // heads, u % heads

    def attn_block(u):
        block, h = place(u)
        rows = pl.ds(pl.multiple_of(block * BLOCK, BLOCK), BLOCK)
        return columns(attn, h, rows)

    def attn_in(u):
        return pltpu.make_async_copy(attn_block(u), stage.at[u % 2], in_sem.at[u % 2])

    def block_out(u):
        if second:
            block, h = place(u)
            rows = pl.ds(pl.multiple_of(block * BLOCK, BLOCK), BLOCK)
            return pltpu.make_async_copy(mstage.at[u % 2], columns(mixed, h, rows), stage_sem.at[u % 2])
        return pltpu.make_async_copy(stage.at[u % 2], attn_block(u), stage_sem.at[u % 2])

    for c in load_weights(0):
        c.start()
    for h in range(heads):
        for i in (0, 1, 2) if second else (0, 1, 2, 3):
            load_one(i, h).start()
    if second:
        attn_in(0).start()
    sq_all[mine] = jnp.zeros(sq_all.shape[1:], jnp.float32)

    @pl.when(gives & jnp.logical_not(works))
    def _():
        @pl.loop(0, g.shape[0])
        def _(n):
            g[n] = jnp.zeros(g.shape[1:], g.dtype)

    if not second:

        @pl.when(me == 0)
        def _():
            @pl.loop(0, heads)
            def _(h):
                kbuf[h, pl.ds(0, WIN)] = jnp.zeros((WIN, hd), kbuf.dtype)
                vbuf[h, pl.ds(0, WIN)] = jnp.zeros((WIN, hd), vbuf.dtype)

    greet(near_size, far_size)

    def halo(h):
        rows = pl.ds(local - WIN, WIN)
        out = []
        for i, (src, dst) in enumerate(((keys, kbuf), (values, vbuf))):
            out.append(
                pltpu.make_async_remote_copy(
                    src_ref=columns(src, h, rows),
                    dst_ref=dst.at[h, pl.ds(0, WIN)],
                    send_sem=halo_send.at[i],
                    recv_sem=halo_recv.at[i, h],
                    device_id={"seq": me + 1},
                    device_id_type=pl.DeviceIdType.MESH,
                )
            )
        return out

    netw = Net(second, near_size, far_size, g, res, acc, got, send, recv)

    def position(rows):
        return anchor + rows + lax.broadcasted_iota(jnp.int32, (BLOCK, 1), 0)

    def backward(h):
        for c in load_weights(h):
            c.wait()
        if second:
            coef = fast_rate / jnp.sqrt(jnp.sum(sq_in[...]) / total_count + epsilon)
        for j in range(3):
            for p in range(pieces):
                rows = pl.ds(p * CHUNK, CHUNK)
                w = wbuf[j, rows]
                if second:
                    w = w - coef * gbuf[j * pieces + p].astype(jnp.float32)
                wb[h, j, rows] = w.astype(jnp.bfloat16)

        @pl.when(h + 1 < heads)
        def _():
            for c in load_weights(h + 1):
                c.start()

        for k in (0, 1):
            load_one(k, h).wait()

        @pl.loop(0, blocks)
        def _(b):
            start = pl.multiple_of(b * BLOCK, BLOCK)
            rows = pl.ds(start, BLOCK)
            x = kbuf[h, pl.ds(pad + start, BLOCK)]
            rate = rate_ref[rows]
            column = lax.broadcasted_iota(jnp.int32, rate.shape, 1)
            scaled = jnp.sum(jnp.where(column == h, rate, 0.0), axis=1, keepdims=True)
            inside = (position(start) >= edge) if second else (position(start) < edge)
            scaled = scaled * jnp.where(inside, 1.0, 0.0)
            first = mm(x, wb[h, 0], 1, 0)
            third = mm(x, wb[h, 1], 1, 0)
            d_out = (-scaled * tbuf[h, rows].astype(jnp.float32)).astype(jnp.bfloat16)
            d_act = mm(d_out, wb[h, 2], 1, 0)
            sigma = jax.nn.sigmoid(first)
            swish = first * sigma
            dbuf[0, rows] = (d_act * third * sigma * (1.0 + first * (1.0 - sigma))).astype(jnp.bfloat16)
            dbuf[1, rows] = (d_act * swish).astype(jnp.bfloat16)
            dbuf[2, rows] = (swish * third).astype(jnp.bfloat16)
            dbuf[3, rows] = d_out

    def outer(h, j):
        left = kbuf[h, pl.ds(pad, local)] if j < 2 else dbuf[3]
        value = mm(left, dbuf[j], 0, 0).astype(jnp.bfloat16)
        for p in range(pieces):
            g[h * per + j * pieces + p] = value[p * CHUNK : (p + 1) * CHUNK]

    def attend(u):
        block, h = place(u)
        start = pl.multiple_of(block * BLOCK, BLOCK)
        slot = u % 2

        @pl.when(block == blocks - 1)
        def _():
            for k in (2, 3):
                load_one(k, h).wait()

            @pl.when(jnp.logical_not(early))
            def _():
                for k in (0, 1):
                    load_one(k, h).wait()

        @pl.when((block == WIN // BLOCK - 1) & (me > 0))
        def _():
            for c in halo(h):
                c.wait_recv()

        @pl.when(u >= 2)
        def _():
            block_out(u - 2).wait()

        span = WIN + BLOCK
        q = qbuf[h, pl.ds(start, BLOCK)]
        scores = mm(q, kbuf[h, pl.ds(start, span)], 1, 1) * (hd ** (-0.5))
        row = lax.broadcasted_iota(jnp.int32, (BLOCK, span), 0)
        colm = lax.broadcasted_iota(jnp.int32, (BLOCK, span), 1)
        back = row + WIN - colm
        live = (back >= 0) & (back < win_ref[h]) & (colm >= WIN - start - anchor)
        scores = jnp.where(live, scores, -1e30)
        peak = jnp.max(scores, axis=1, keepdims=True)
        expo = jnp.exp(scores - peak)
        probs = (expo * (1.0 / jnp.sum(expo, axis=1, keepdims=True))).astype(jnp.bfloat16)
        stage[slot] = mm(probs, vbuf[h, pl.ds(start, span)], 1, 0)

        @pl.when(early)
        def _():
            y = fast_output(q, wb, h)
            stage[slot] += jnp.where(position(start) < edge, y, 0.0)

        block_out(u).start()

    def combine(u):
        block, h = place(u)
        start = pl.multiple_of(block * BLOCK, BLOCK)
        slot = u % 2

        @pl.when(u + 1 < units)
        def _():
            attn_in(u + 1).start()

        attn_in(u).wait()

        @pl.when(block == blocks - 1)
        def _():
            load_one(2, h).wait()

            @pl.when(jnp.logical_not(late))
            def _():
                for k in (0, 1):
                    load_one(k, h).wait()

        @pl.when(u >= 2)
        def _():
            block_out(u - 2).wait()

        @pl.when(late)
        def _():
            y = fast_output(qbuf[h, pl.ds(start, BLOCK)], wb, h)
            mstage[slot] = (stage[slot] + jnp.where(position(start) >= edge, y, 0.0)).astype(jnp.bfloat16)

        @pl.when(jnp.logical_not(late))
        def _():
            mstage[slot] = stage[slot].astype(jnp.bfloat16)

        block_out(u).start()

    def put(n):
        return pltpu.make_async_copy(res.at[n], sums.at[n], out_sem.at[0])

    def finish(n):
        put(n).start()
        part = jnp.square(res[n].astype(jnp.float32))
        sq_all[mine] += jnp.sum(part.reshape(-1, *sq_all.shape[1:]), axis=0)

    @pl.loop(0, max(netw.length, begin + units))
    def _(i):
        h = i // per

        if not second:

            @pl.when((i % HALO_EVERY == 0) & (i // HALO_EVERY < heads) & (me < count - 1))
            def _():
                for c in halo(i // HALO_EVERY):
                    c.start()

        @pl.when((h < heads) & works)
        def _():
            for j in range(3):

                @pl.when(i % per == j * pieces)
                def _():
                    if j == 0:
                        backward(h)
                    outer(h, j)

        netw.advance(i, finish)
        u = i - begin

        @pl.when((u >= 0) & (u < units))
        def _():
            (combine if second else attend)(u)

    netw.drain()
    share_squares(sq_all, sq_ref, sq_send, sq_recv)
    if not second:

        @pl.when(me < count - 1)
        def _():
            for i, buf in enumerate((kbuf, vbuf)):
                every = buf.at[pl.ds(0, heads), pl.ds(0, WIN)]
                pltpu.make_async_remote_copy(
                    src_ref=every, dst_ref=every, send_sem=halo_send.at[i], recv_sem=halo_recv.at[i, 0],
                    device_id={"seq": me + 1}, device_id_type=pl.DeviceIdType.MESH,
                ).wait_send()

    @pl.when(jnp.logical_not(works))
    def _():
        for c in load_weights(0):
            c.wait()

    for u in (units - 2, units - 1):
        block_out(u).wait()
    pltpu.make_async_copy(res, sums, out_sem.at[0]).wait()


def block_step(second, arrays, total_count):
    near, far = sizes_of_seq()
    if second:
        edge, rate, sq_in, keys, queries, targets, weights, g_in, attn = arrays
    else:
        edge, window, rate, keys, values, queries, targets, weights = arrays
    heads, _, hd, hid = weights.shape
    local = keys.shape[0]
    chunks = heads * 3 * hd // CHUNK
    vmem = pl.BlockSpec(memory_space=pltpu.VMEM)
    smem = pl.BlockSpec(memory_space=pltpu.SMEM)
    hbm = pl.BlockSpec(memory_space=pl.ANY)
    half = CHUNK // CORES
    kinds = link_kinds(near)
    ranks = lax.axis_size("head")
    dma = pltpu.SemaphoreType.DMA
    bf16, f32 = jnp.bfloat16, jnp.float32
    pad = 0 if second else WIN
    scratch = [
        pltpu.VMEM((heads, pad + local, hd), bf16),
        pltpu.VMEM((heads, local, hd), bf16),
        pltpu.VMEM((heads, local, hd), bf16),
        pltpu.VMEM((3, hd, hid), f32),
        pltpu.VMEM((heads, 3, hd, hid), bf16),
        pltpu.VMEM((chunks, CHUNK, hid), bf16),
        pltpu.VMEM((chunks, CHUNK, hid), bf16),
        pltpu.VMEM((chunks, half, hid), bf16),
        pltpu.VMEM((3, chunks, half, hid), bf16),
        pltpu.VMEM((4, local, hd), bf16),
        pltpu.VMEM((2, BLOCK, hd), f32),
        pltpu.VMEM((ranks, 8, hid), f32),
        dma((kinds,)),
        dma((kinds, chunks)),
        dma((ranks,)),
        dma((ranks,)),
        dma((4, heads)),
        dma((2,)),
        dma((1,)),
        dma((2,)),
    ]
    if second:
        scratch += [pltpu.VMEM((3 * hd // CHUNK, CHUNK, hid), bf16), pltpu.VMEM((2, BLOCK, hd), bf16), dma((2,))]
        in_specs = [smem, vmem, vmem, hbm, hbm, hbm, hbm, hbm, hbm]
        wide = jax.ShapeDtypeStruct(keys.shape, bf16)
    else:
        scratch += [pltpu.VMEM((heads, pad + local, hd), bf16), dma((2,)), dma((2, heads))]
        in_specs = [smem, smem, vmem, hbm, hbm, hbm, hbm, hbm]
        wide = jax.ShapeDtypeStruct(keys.shape, f32)
    return pl.pallas_call(
        functools.partial(block_kernel, second, near, far, total_count),
        in_specs=in_specs,
        out_specs=(hbm, vmem, hbm),
        out_shape=(
            jax.ShapeDtypeStruct((chunks, CHUNK, hid), bf16),
            jax.ShapeDtypeStruct((8, hid), f32),
            wide,
        ),
        scratch_shapes=scratch,
        compiler_params=pltpu.CompilerParams(
            collective_id=int(second), has_side_effects=True, vmem_limit_bytes=67043328
        ),
        cost_estimate=pl.CostEstimate(flops=10**11, bytes_accessed=60 << 20, transcendentals=0),
        name="second" if second else "first",
    )(*arrays)


def renew_kernel(total_count, sq0_ref, sq1_ref, w_ref, g0_ref, g1_ref, out_ref):
    coef = [
        fast_rate / jnp.sqrt(jnp.sum(s[...]) / total_count + epsilon) for s in (sq0_ref, sq1_ref)
    ]
    out_ref[...] = (
        w_ref[...] - coef[0] * g0_ref[...].astype(jnp.float32) - coef[1] * g1_ref[...].astype(jnp.float32)
    )


def renew(total_count, sq0, sq1, weights, g0, g1):
    rows = 3 * weights.shape[2]
    flat = (-1, weights.shape[-1])
    w = weights.reshape(flat)
    small = pl.BlockSpec(sq0.shape, lambda i: (0, 0))
    tile = pl.BlockSpec((rows, w.shape[1]), lambda i: (i, 0))
    return pl.pallas_call(
        functools.partial(renew_kernel, total_count),
        grid=(w.shape[0] // rows,),
        in_specs=[small, small, tile, tile, tile],
        out_specs=tile,
        out_shape=jax.ShapeDtypeStruct(w.shape, jnp.float32),
        compiler_params=pltpu.CompilerParams(vmem_limit_bytes=40 << 20),
        cost_estimate=pl.CostEstimate(flops=4 * w.size, bytes_accessed=12 * w.size, transcendentals=0),
        name="renew",
    )(sq0, sq1, w, g0.reshape(flat), g1.reshape(flat)).reshape(weights.shape)


def per_device(queries, keys, values, targets, token_rate, window, split, fast_init):
    total_count = float(fast_init.size * lax.axis_size("head"))
    g0, sq0, attn = block_step(
        False, (split, window, token_rate, keys, values, queries, targets, fast_init), total_count
    )
    g1, sq1, mixed = block_step(
        True, (split, token_rate, sq0, keys, queries, targets, fast_init, g0, attn), total_count
    )
    return mixed, renew(total_count, sq0, sq1, fast_init, g0, g1)


def solution(mesh):
    return jax.shard_map(
        per_device,
        mesh=mesh,
        in_specs=(
            P("seq", "head"),
            P("seq", "head"),
            P("seq", "head"),
            P("seq", "head"),
            P("seq", "head"),
            P("head"),
            P(),
            P("head", None, None, None),
        ),
        out_specs=(P("seq", "head"), P("head", None, None, None)),
        check_vma=False,
    )
```

profile of v0, /device:TPU:0, one launch (start us, length us, event | category | flops | bytes accessed | tf_op | source)
XLA Modules:
  0.0 254.5 jit_solution(4404535543533530808)
XLA Ops:
  1.3 1.6 copy.11.refs_2_.refs_1_
  2.9 136.8 %first.1 = (bf16[24,256,512]{2,1,0:T(8,128)(2,1)}, f32[8,512]{1,0:T(8,128)}, f32[768,2048]{1,0:T(8,128)}) custom-call(s32[1]{0:T(128)S(6)} %copy.13.refs_0_, s32[4]{0:T(128)} %refs_1_.2, f32[768,4]{1,0:T(8,128)} %copy.11.refs_2_.refs_1_, bf16[768,2048]{1,0:T(8,128)(2,1)} %refs_3_.3, bf16[768,2048]{1,0:T(8,128)(2,1)} %refs_4_.2, bf16[768,2048]{1,0:T(8,128)(2,1)} %refs_4_.3, ...), custom_call_target="tpu_custom_call" | custom-call | flops 99999997952 | bytes 62914560 | tf_op jit(solution)/shard_map/first/pallas_call | solution.py:756
  139.7 93.8 %second.1 = (bf16[24,256,512]{2,1,0:T(8,128)(2,1)}, f32[8,512]{1,0:T(8,128)}, bf16[768,2048]{1,0:T(8,128)(2,1)}) custom-call(s32[1]{0:T(128)S(6)} %copy.13.refs_0_, f32[768,4]{1,0:T(8,128)} %copy.11.refs_2_.refs_1_, f32[8,512]{1,0:T(8,128)} %get-tuple-element.8.refs_2_.sq0_ref, bf16[768,2048]{1,0:T(8,128)(2,1)} %refs_3_.3, bf16[768,2048]{1,0:T(8,128)(2,1)} %refs_4_.3, ...), custom_call_target="tpu_custom_call" | custom-call | flops 99999997952 | bytes 62914560 | tf_op jit(solution)/shard_map/second/pallas_call | solution.py:756
  233.6 0.0 copy-start
  233.6 2.8 %copy-done = bf16[24,256,512]{2,1,0:T(8,128)(2,1)S(1)} copy-done((bf16[24,256,512]{2,1,0:T(8,128)(2,1)S(1)}, bf16[24,256,512]{2,1,0:T(8,128)(2,1)}, u32[]{:S(2)}) %copy-start) | copy-done | bytes 6291480
  236.4 0.0 copy-start.1
  236.4 2.8 %copy-done.1 = bf16[24,256,512]{2,1,0:T(8,128)(2,1)S(1)} copy-done((bf16[24,256,512]{2,1,0:T(8,128)(2,1)S(1)}, bf16[24,256,512]{2,1,0:T(8,128)(2,1)}, u32[]{:S(2)}) %copy-start.1) | copy-done | bytes 6291480
  239.2 0.0 copy-start.2
  239.2 0.7 copy-done.2
  239.9 0.0 copy-start.3
  239.9 0.7 copy-done.3
  240.6 0.0 copy-start.4
  240.6 12.3 %renew.1 = f32[6144,512]{1,0:T(8,128)} custom-call(f32[8,512]{1,0:T(8,128)S(1)} %copy-done.2, f32[8,512]{1,0:T(8,128)S(1)} %copy-done.3, f32[6144,512]{1,0:T(8,128)} %bitcast.6, bf16[6144,512]{1,0:T(8,128)(2,1)S(1)} %bitcast.4, bf16[6144,512]{1,0:T(8,128)(2,1)S(1)} %bitcast.5), custom_call_target="tpu_custom_call" | custom-call | flops 12582912 | bytes 37748736 | tf_op jit(solution)/shard_map/renew/pallas_call | solution.py:789
  252.9 0.0 copy-done.4
  252.9 1.7 copy.14
Async XLA Ops:
  233.6 2.8 %copy-start = (bf16[24,256,512]{2,1,0:T(8,128)(2,1)S(1)}, bf16[24,256,512]{2,1,0:T(8,128)(2,1)}, u32[]{:S(2)}) copy-start(bf16[24,256,512]{2,1,0:T(8,128)(2,1)} %get-tuple-element.9.refs_7_) | copy-start | bytes 18874372
  236.4 2.8 %copy-start.1 = (bf16[24,256,512]{2,1,0:T(8,128)(2,1)S(1)}, bf16[24,256,512]{2,1,0:T(8,128)(2,1)}, u32[]{:S(2)}) copy-start(bf16[24,256,512]{2,1,0:T(8,128)(2,1)} %get-tuple-element.13) | copy-start | bytes 18874372
  239.2 0.7 copy-start.2
  239.9 0.7 copy-start.3
  240.6 12.3 %copy-start.4 = (bf16[768,2048]{1,0:T(8,128)(2,1)S(1)}, bf16[768,2048]{1,0:T(8,128)(2,1)}, u32[]{:S(2)}) copy-start(bf16[768,2048]{1,0:T(8,128)(2,1)} %get-tuple-element.16) | copy-start | bytes 9437188
where the time goes:
time: 255 us
  Pallas kernels  243 us (95%)
  local copies, waits for them, and re-layouts  10.3 us (4%)
    pallas_call x2, Pallas kernels, block_step(): pl.pallas_call(functools.partial(block_kernel, second, near, far, total_c...  231 us
    pallas_call x1, Pallas kernels, renew(): pl.pallas_call(functools.partial(renew_kernel, total_count), grid=(w.shap...  12.3 us
    unnamed x12, local copies, waits for them, and re-layouts  10.3 us

commit v1 on v0

--- a/solution.py
+++ b/solution.py
@@ -19,8 +19,8 @@
     )
 
 
-SHARES = (8, 4, 4)
-STEPS = (1, 2, 2)
+SHARES = ((8, 4, 4), (8, 4, 4))
+STEPS = ((1, 2, 2), (1, 2, 2))
 CHUNK = 256
 
 
@@ -79,7 +79,7 @@
         line = far_size - 1 - far if mirror else far
         last = (5 * far_size - 1) // 8
         gives = line <= last
-        step_core, step_near, step_line = STEPS
+        step_core, step_near, step_line = STEPS[mirror]
 
         def device(line_to, near_to, core_to):
             far_to = far_size - 1 - line_to if mirror else line_to
@@ -107,8 +107,9 @@
         )
         self.stage(0, swap.start)
 
-        unit = half // sum(SHARES)
-        count = [s * unit for s in SHARES]
+        shares = SHARES[mirror]
+        unit = half // sum(shares)
+        count = [s * unit for s in shares]
         first = [sum(count[:i]) for i in range(3)]
         mid = last // 2
         ends = []
@@ -332,7 +333,11 @@
 
 
 BLOCK = 256
-HALO_EVERY = 5
+RENEW_STEPS = 4
+HALO_PIECES = 8
+HALO_LEAD = 4
+NEAR_AT = 19
+NEAR_EVERY = 2
 
 
 def sizes_of_seq():
@@ -402,19 +407,19 @@
         return out
 
     if second:
-        edge_ref, rate_ref, sq_in, keys, queries, targets, weights, g_in, attn = take(9)
+        edge_ref, win_ref, rate_ref, sq_in, keys, values, queries, targets, weights = take(9)
+        g_in, attn, k_far, v_far = take(4)
         sums, sq_ref, mixed = take(3)
     else:
         edge_ref, win_ref, rate_ref, keys, values, queries, targets, weights = take(8)
-        sums, sq_ref, attn = take(3)
+        sums, sq_ref, attn, k_far, v_far = take(5)
     kbuf, qbuf, tbuf, wbuf, wb, g, res, acc, got, dbuf, stage, sq_all = take(12)
     send, recv, sq_send, sq_recv, load, wload, out_sem, stage_sem = take(8)
     if second:
-        gbuf, mstage, in_sem = take(3)
-        pad = 0
+        vbuf, gbuf, mstage, in_sem, far_sem = take(5)
     else:
-        vbuf, halo_send, halo_recv = take(3)
-        pad = WIN
+        vbuf, halo_send, halo_recv, far_sem = take(4)
+    pad = WIN
     assert not refs
 
     heads = weights.shape[0]
@@ -434,6 +439,33 @@
     blocks = local // BLOCK
     units = blocks * heads
     begin = (heads - 1) * (per - 1)
+    ahead = per - 3
+    assert blocks % ahead == 0
+    halo_blocks = WIN // BLOCK
+    plain = (blocks - halo_blocks) * heads
+    here = heads - heads // 2
+
+    def far_copies(h):
+        k = h - here
+        pairs = [(kbuf.at[h, pl.ds(0, WIN)], k_far.at[k]), (vbuf.at[k if second else h, pl.ds(0, WIN)], v_far.at[k])]
+        if second:
+            pairs = [(b, a) for a, b in pairs]
+            rows = pl.ds(0, WIN)
+            pairs.append((columns(values, h, rows), vbuf.at[k, pl.ds(WIN, WIN)]))
+        return [pltpu.make_async_copy(a, b, far_sem.at[i, k]) for i, (a, b) in enumerate(pairs)]
+
+    def attention(q, v_all, h, start):
+        span = WIN + BLOCK
+        scores = mm(q, kbuf[h, pl.ds(start, span)], 1, 1) * (hd ** (-0.5))
+        row = lax.broadcasted_iota(jnp.int32, (BLOCK, span), 0)
+        colm = lax.broadcasted_iota(jnp.int32, (BLOCK, span), 1)
+        back = row + WIN - colm
+        live = (back >= 0) & (back < win_ref[h]) & (colm >= WIN - start - anchor)
+        scores = jnp.where(live, scores, -1e30)
+        peak = jnp.max(scores, axis=1, keepdims=True)
+        expo = jnp.exp(scores - peak)
+        probs = (expo * (1.0 / jnp.sum(expo, axis=1, keepdims=True))).astype(jnp.bfloat16)
+        return mm(probs, v_all[pl.ds(start, span)], 1, 0)
     edge = edge_ref[0]
 
     def columns(ref, h, rows=None):
@@ -457,20 +489,15 @@
     def place(u):
         return blocks - 1 - u // heads, u % heads
 
-    def attn_block(u):
-        block, h = place(u)
-        rows = pl.ds(pl.multiple_of(block * BLOCK, BLOCK), BLOCK)
-        return columns(attn, h, rows)
+    def block_of(ref, block, h):
+        return columns(ref, h, pl.ds(pl.multiple_of(block * BLOCK, BLOCK), BLOCK))
 
     def attn_in(u):
-        return pltpu.make_async_copy(attn_block(u), stage.at[u % 2], in_sem.at[u % 2])
-
-    def block_out(u):
-        if second:
-            block, h = place(u)
-            rows = pl.ds(pl.multiple_of(block * BLOCK, BLOCK), BLOCK)
-            return pltpu.make_async_copy(mstage.at[u % 2], columns(mixed, h, rows), stage_sem.at[u % 2])
-        return pltpu.make_async_copy(stage.at[u % 2], attn_block(u), stage_sem.at[u % 2])
+        return pltpu.make_async_copy(block_of(attn, *place(u)), stage.at[u % 2], in_sem.at[u % 2])
+
+    def block_out(block, h, slot):
+        src, dst = (mstage, mixed) if second else (stage, attn)
+        return pltpu.make_async_copy(src.at[slot], block_of(dst, block, h), stage_sem.at[slot])
 
     for c in load_weights(0):
         c.start()
@@ -479,6 +506,9 @@
             load_one(i, h).start()
     if second:
         attn_in(0).start()
+        for h in range(here, heads):
+            for c in far_copies(h):
+                c.start()
     sq_all[mine] = jnp.zeros(sq_all.shape[1:], jnp.float32)
 
     @pl.when(gives & jnp.logical_not(works))
@@ -498,14 +528,14 @@
 
     greet(near_size, far_size)
 
-    def halo(h):
-        rows = pl.ds(local - WIN, WIN)
+    def halo(h, first=0, size=WIN):
+        rows = pl.ds(pl.multiple_of(local - WIN + first, 16), size)
         out = []
         for i, (src, dst) in enumerate(((keys, kbuf), (values, vbuf))):
             out.append(
                 pltpu.make_async_remote_copy(
                     src_ref=columns(src, h, rows),
-                    dst_ref=dst.at[h, pl.ds(0, WIN)],
+                    dst_ref=dst.at[h, pl.ds(first, size)],
                     send_sem=halo_send.at[i],
                     recv_sem=halo_recv.at[i, h],
                     device_id={"seq": me + 1},
@@ -519,7 +549,7 @@
     def position(rows):
         return anchor + rows + lax.broadcasted_iota(jnp.int32, (BLOCK, 1), 0)
 
-    def backward(h):
+    def prepare(h):
         for c in load_weights(h):
             c.wait()
         if second:
@@ -537,17 +567,21 @@
             for c in load_weights(h + 1):
                 c.start()
 
-        for k in (0, 1):
-            load_one(k, h).wait()
-
-        @pl.loop(0, blocks)
-        def _(b):
+    def backward(h, kind):
+        @pl.when(kind == 0)
+        def _():
+            for k in (0, 1):
+                load_one(k, h).wait()
+
+        for turn in range(0, blocks, ahead):
+            b = kind + turn
             start = pl.multiple_of(b * BLOCK, BLOCK)
             rows = pl.ds(start, BLOCK)
             x = kbuf[h, pl.ds(pad + start, BLOCK)]
-            rate = rate_ref[rows]
-            column = lax.broadcasted_iota(jnp.int32, rate.shape, 1)
-            scaled = jnp.sum(jnp.where(column == h, rate, 0.0), axis=1, keepdims=True)
+            rate = rate_ref[pl.ds(h, 1), rows]
+            down = lax.broadcasted_iota(jnp.int32, (BLOCK, BLOCK), 0)
+            across = lax.broadcasted_iota(jnp.int32, (BLOCK, BLOCK), 1)
+            scaled = jnp.sum(jnp.where(down == across, rate, 0.0), axis=1, keepdims=True)
             inside = (position(start) >= edge) if second else (position(start) < edge)
             scaled = scaled * jnp.where(inside, 1.0, 0.0)
             first = mm(x, wb[h, 0], 1, 0)
@@ -567,10 +601,9 @@
         for p in range(pieces):
             g[h * per + j * pieces + p] = value[p * CHUNK : (p + 1) * CHUNK]
 
-    def attend(u):
-        block, h = place(u)
+    def attend(block, h, order):
         start = pl.multiple_of(block * BLOCK, BLOCK)
-        slot = u % 2
+        slot = order % 2
 
         @pl.when(block == blocks - 1)
         def _():
@@ -582,34 +615,32 @@
                 for k in (0, 1):
                     load_one(k, h).wait()
 
-        @pl.when((block == WIN // BLOCK - 1) & (me > 0))
+        @pl.when((block == halo_blocks - 1) & (h < here) & (me > 0))
         def _():
             for c in halo(h):
                 c.wait_recv()
 
-        @pl.when(u >= 2)
-        def _():
-            block_out(u - 2).wait()
-
-        span = WIN + BLOCK
+        @pl.when(order >= 2)
+        def _():
+            block_out(block, h, slot).wait()
+
         q = qbuf[h, pl.ds(start, BLOCK)]
-        scores = mm(q, kbuf[h, pl.ds(start, span)], 1, 1) * (hd ** (-0.5))
-        row = lax.broadcasted_iota(jnp.int32, (BLOCK, span), 0)
-        colm = lax.broadcasted_iota(jnp.int32, (BLOCK, span), 1)
-        back = row + WIN - colm
-        live = (back >= 0) & (back < win_ref[h]) & (colm >= WIN - start - anchor)
-        scores = jnp.where(live, scores, -1e30)
-        peak = jnp.max(scores, axis=1, keepdims=True)
-        expo = jnp.exp(scores - peak)
-        probs = (expo * (1.0 / jnp.sum(expo, axis=1, keepdims=True))).astype(jnp.bfloat16)
-        stage[slot] = mm(probs, vbuf[h, pl.ds(start, span)], 1, 0)
+        inside = (block >= halo_blocks) | (h < here)
+
+        @pl.when(inside)
+        def _():
+            stage[slot] = attention(q, vbuf.at[h], h, start)
+
+        @pl.when(jnp.logical_not(inside))
+        def _():
+            stage[slot] = jnp.zeros(stage.shape[1:], jnp.float32)
 
         @pl.when(early)
         def _():
             y = fast_output(q, wb, h)
             stage[slot] += jnp.where(position(start) < edge, y, 0.0)
 
-        block_out(u).start()
+        block_out(block, h, slot).start()
 
     def combine(u):
         block, h = place(u)
@@ -633,7 +664,19 @@
 
         @pl.when(u >= 2)
         def _():
-            block_out(u - 2).wait()
+            block_out(block, h, slot).wait()
+
+        if here < heads:
+
+            @pl.when((block == halo_blocks - 1) & (h >= here))
+            def _():
+                for c in far_copies(h):
+                    c.wait()
+
+            @pl.when((block < halo_blocks) & (h >= here))
+            def _():
+                q = qbuf[h, pl.ds(start, BLOCK)]
+                stage[slot] += attention(q, vbuf.at[h - here], h, start)
 
         @pl.when(late)
         def _():
@@ -644,7 +687,7 @@
         def _():
             mstage[slot] = stage[slot].astype(jnp.bfloat16)
 
-        block_out(u).start()
+        block_out(block, h, slot).start()
 
     def put(n):
         return pltpu.make_async_copy(res.at[n], sums.at[n], out_sem.at[0])
@@ -654,37 +697,99 @@
         part = jnp.square(res[n].astype(jnp.float32))
         sq_all[mine] += jnp.sum(part.reshape(-1, *sq_all.shape[1:]), axis=0)
 
-    @pl.loop(0, max(netw.length, begin + units))
+    def gradient(i):
+        h = i // per
+        kind = i % per
+
+        @pl.when(h < heads)
+        def _():
+            @pl.when(kind < ahead)
+            def _():
+                backward(h, kind)
+
+            for j in range(3):
+
+                @pl.when(kind == ahead + j)
+                def _():
+                    outer(h, j)
+
+        @pl.when((h < heads - 1) & (kind == per - 1))
+        def _():
+            prepare(h + 1)
+
+    def send_halo(i):
+        size = WIN // HALO_PIECES
+
+        @pl.when((i < heads * HALO_PIECES) & (me < count - 1))
+        def _():
+            for c in halo(i // HALO_PIECES, pl.multiple_of((i % HALO_PIECES) * size, size), size):
+                c.start()
+
+    if not second:
+
+        @pl.loop(0, HALO_LEAD)
+        def _(i):
+            send_halo(i)
+
+    @pl.when(works)
+    def _():
+        prepare(0)
+
+        @pl.loop(0, ahead)
+        def _(i):
+            gradient(i)
+
+    if second:
+        steps = [begin + units]
+    else:
+        near_at = max(NEAR_AT, begin + plain)
+        steps = [begin + plain, near_at + NEAR_EVERY * (units - plain)]
+
+    @pl.loop(0, max(netw.length, *steps))
     def _(i):
-        h = i // per
-
         if not second:
-
-            @pl.when((i % HALO_EVERY == 0) & (i // HALO_EVERY < heads) & (me < count - 1))
-            def _():
-                for c in halo(i // HALO_EVERY):
-                    c.start()
-
-        @pl.when((h < heads) & works)
-        def _():
-            for j in range(3):
-
-                @pl.when(i % per == j * pieces)
-                def _():
-                    if j == 0:
-                        backward(h)
-                    outer(h, j)
+            send_halo(i + HALO_LEAD)
+
+        @pl.when(works)
+        def _():
+            gradient(i + ahead)
 
         netw.advance(i, finish)
         u = i - begin
-
-        @pl.when((u >= 0) & (u < units))
-        def _():
-            (combine if second else attend)(u)
+        if second:
+
+            @pl.when((u >= 0) & (u < units))
+            def _():
+                combine(u)
+        else:
+
+            @pl.when((u >= 0) & (u < plain))
+            def _():
+                block, h = place(u)
+                attend(block, h, u)
+
+            v = i - near_at
+            w = v // NEAR_EVERY
+
+            @pl.when((v >= 0) & (v % NEAR_EVERY == 0) & (w < units - plain))
+            def _():
+                attend(halo_blocks - 1 - w % halo_blocks, w // halo_blocks, plain + w)
 
     netw.drain()
     share_squares(sq_all, sq_ref, sq_send, sq_recv)
     if not second:
+        for h in range(here, heads):
+
+            @pl.when(me > 0)
+            def _():
+                for c in halo(h):
+                    c.wait_recv()
+
+            for c in far_copies(h):
+                c.start()
+        for h in range(here, heads):
+            for c in far_copies(h):
+                c.wait()
 
         @pl.when(me < count - 1)
         def _():
@@ -700,17 +805,17 @@
         for c in load_weights(0):
             c.wait()
 
-    for u in (units - 2, units - 1):
-        block_out(u).wait()
+    for slot in range(2):
+        block_out(0, 0, slot).wait()
     pltpu.make_async_copy(res, sums, out_sem.at[0]).wait()
 
 
 def block_step(second, arrays, total_count):
     near, far = sizes_of_seq()
     if second:
-        edge, rate, sq_in, keys, queries, targets, weights, g_in, attn = arrays
+        keys, weights = arrays[4], arrays[8]
     else:
-        edge, window, rate, keys, values, queries, targets, weights = arrays
+        keys, weights = arrays[3], arrays[7]
     heads, _, hd, hid = weights.shape
     local = keys.shape[0]
     chunks = heads * 3 * hd // CHUNK
@@ -722,7 +827,9 @@
     ranks = lax.axis_size("head")
     dma = pltpu.SemaphoreType.DMA
     bf16, f32 = jnp.bfloat16, jnp.float32
-    pad = 0 if second else WIN
+    pad = WIN
+    away = heads // 2
+    far_shape = (max(away, 1), WIN, hd)
     scratch = [
         pltpu.VMEM((heads, pad + local, hd), bf16),
         pltpu.VMEM((heads, local, hd), bf16),
@@ -746,22 +853,36 @@
         dma((2,)),
     ]
     if second:
-        scratch += [pltpu.VMEM((3 * hd // CHUNK, CHUNK, hid), bf16), pltpu.VMEM((2, BLOCK, hd), bf16), dma((2,))]
-        in_specs = [smem, vmem, vmem, hbm, hbm, hbm, hbm, hbm, hbm]
+        scratch += [
+            pltpu.VMEM((max(away, 1), 2 * WIN, hd), bf16),
+            pltpu.VMEM((3 * hd // CHUNK, CHUNK, hid), bf16),
+            pltpu.VMEM((2, BLOCK, hd), bf16),
+            dma((2,)),
+            dma((3, max(away, 1))),
+        ]
+        in_specs = [smem, smem, vmem, vmem] + [hbm] * 9
+        more = ()
         wide = jax.ShapeDtypeStruct(keys.shape, bf16)
     else:
-        scratch += [pltpu.VMEM((heads, pad + local, hd), bf16), dma((2,)), dma((2, heads))]
+        scratch += [
+            pltpu.VMEM((heads, pad + local, hd), bf16),
+            dma((2,)),
+            dma((2, heads)),
+            dma((2, max(away, 1))),
+        ]
+        more = (jax.ShapeDtypeStruct(far_shape, bf16),) * 2
         in_specs = [smem, smem, vmem, hbm, hbm, hbm, hbm, hbm]
         wide = jax.ShapeDtypeStruct(keys.shape, f32)
     return pl.pallas_call(
         functools.partial(block_kernel, second, near, far, total_count),
         in_specs=in_specs,
-        out_specs=(hbm, vmem, hbm),
+        out_specs=(hbm, vmem, hbm) + (hbm,) * len(more),
         out_shape=(
             jax.ShapeDtypeStruct((chunks, CHUNK, hid), bf16),
             jax.ShapeDtypeStruct((8, hid), f32),
             wide,
-        ),
+        )
+        + more,
         scratch_shapes=scratch,
         compiler_params=pltpu.CompilerParams(
             collective_id=int(second), has_side_effects=True, vmem_limit_bytes=67043328
@@ -771,42 +892,50 @@
     )(*arrays)
 
 
-def renew_kernel(total_count, sq0_ref, sq1_ref, w_ref, g0_ref, g1_ref, out_ref):
+def renew_kernel(total_count, sq0_ref, sq1_ref, w_ref, g0_ref, g1_ref, mixed_ref, out_ref, copy_ref):
     coef = [
         fast_rate / jnp.sqrt(jnp.sum(s[...]) / total_count + epsilon) for s in (sq0_ref, sq1_ref)
     ]
     out_ref[...] = (
         w_ref[...] - coef[0] * g0_ref[...].astype(jnp.float32) - coef[1] * g1_ref[...].astype(jnp.float32)
     )
-
-
-def renew(total_count, sq0, sq1, weights, g0, g1):
-    rows = 3 * weights.shape[2]
+    copy_ref[...] = mixed_ref[...]
+
+
+def renew(total_count, sq0, sq1, weights, g0, g1, mixed):
     flat = (-1, weights.shape[-1])
     w = weights.reshape(flat)
+    steps = RENEW_STEPS
     small = pl.BlockSpec(sq0.shape, lambda i: (0, 0))
-    tile = pl.BlockSpec((rows, w.shape[1]), lambda i: (i, 0))
-    return pl.pallas_call(
+    tile = pl.BlockSpec((w.shape[0] // steps, w.shape[1]), lambda i: (i, 0))
+    rows = pl.BlockSpec((mixed.shape[0] // steps, mixed.shape[1]), lambda i: (i, 0))
+    out, mixed = pl.pallas_call(
         functools.partial(renew_kernel, total_count),
-        grid=(w.shape[0] // rows,),
-        in_specs=[small, small, tile, tile, tile],
-        out_specs=tile,
-        out_shape=jax.ShapeDtypeStruct(w.shape, jnp.float32),
-        compiler_params=pltpu.CompilerParams(vmem_limit_bytes=40 << 20),
-        cost_estimate=pl.CostEstimate(flops=4 * w.size, bytes_accessed=12 * w.size, transcendentals=0),
+        grid=(steps,),
+        in_specs=[small, small, tile, tile, tile, rows],
+        out_specs=(tile, rows),
+        out_shape=(
+            jax.ShapeDtypeStruct(w.shape, jnp.float32),
+            jax.ShapeDtypeStruct(mixed.shape, mixed.dtype),
+        ),
+        compiler_params=pltpu.CompilerParams(vmem_limit_bytes=67043328),
+        cost_estimate=pl.CostEstimate(flops=4 * w.size, bytes_accessed=16 * w.size, transcendentals=0),
         name="renew",
-    )(sq0, sq1, w, g0.reshape(flat), g1.reshape(flat)).reshape(weights.shape)
+    )(sq0, sq1, w, g0.reshape(flat), g1.reshape(flat), mixed)
+    return mixed, out.reshape(weights.shape)
 
 
 def per_device(queries, keys, values, targets, token_rate, window, split, fast_init):
     total_count = float(fast_init.size * lax.axis_size("head"))
-    g0, sq0, attn = block_step(
-        False, (split, window, token_rate, keys, values, queries, targets, fast_init), total_count
+    g0, sq0, attn, k_far, v_far = block_step(
+        False, (split, window, token_rate.T, keys, values, queries, targets, fast_init), total_count
     )
     g1, sq1, mixed = block_step(
-        True, (split, token_rate, sq0, keys, queries, targets, fast_init, g0, attn), total_count
+        True,
+        (split, window, token_rate.T, sq0, keys, values, queries, targets, fast_init, g0, attn, k_far, v_far),
+        total_count,
     )
-    return mixed, renew(total_count, sq0, sq1, fast_init, g0, g1)
+    return renew(total_count, sq0, sq1, fast_init, g0, g1, mixed)
 
 
 def solution(mesh):

time: 255 us -> 235 us (0.922)
  local copies, waits for them, and re-layouts: 10.3 us -> 0 us
  Pallas kernels: 243 us -> 234 us
    pallas_call x2, Pallas kernels: 231 us -> 217 us  [block_step(): pl.pallas_call(functools.partial(block_kernel, second, near, far, total_c...]
    unnamed x12 -> x0, local copies, waits for them, and re-layouts: 10.3 us -> none
    pallas_call x1, Pallas kernels: 12.3 us -> 16.8 us  [renew(): pl.pallas_call(functools.partial(renew_kernel, total_count), grid=(steps,...]
where the time goes in v1:
time: 235 us
  Pallas kernels  234 us (100%)
    pallas_call x2, Pallas kernels, block_step(): pl.pallas_call(functools.partial(block_kernel, second, near, far, total_c...  217 us
    pallas_call x1, Pallas kernels, renew(): pl.pallas_call(functools.partial(renew_kernel, total_count), grid=(steps,...  16.8 us

profile of v1, /device:TPU:0, one launch (start us, length us, event | category | flops | bytes accessed | tf_op | source)
XLA Modules:
  0.0 235.1 jit_solution(5158308195445672687)
XLA Ops:
  1.3 128.3 %first.1 = (bf16[24,256,512]{2,1,0:T(8,128)(2,1)}, f32[8,512]{1,0:T(8,128)}, f32[768,2048]{1,0:T(8,128)}, bf16[2,512,512]{2,1,0:T(8,128)(2,1)}, bf16[2,512,512]{2,1,0:T(8,128)(2,1)}) custom-call(s32[1]{0:T(128)S(6)} %copy.10.refs_0_, s32[4]{0:T(128)} %refs_1_.3, f32[4,768]{1,0:T(4,128)} %bitcast.9, bf16[768,2048]{1,0:T(8,128)(2,1)} %refs_4_.3, ...), custom_call_target="tpu_custom_call" | custom-call | flops 99999997952 | bytes 62914560 | tf_op jit(solution)/shard_map/first/pallas_call | solution.py:876
  129.6 88.8 %second.1 = (bf16[24,256,512]{2,1,0:T(8,128)(2,1)}, f32[8,512]{1,0:T(8,128)}, bf16[768,2048]{1,0:T(8,128)(2,1)}) custom-call(s32[1]{0:T(128)S(6)} %copy.10.refs_0_, s32[4]{0:T(128)} %refs_1_.3, f32[4,768]{1,0:T(4,128)} %bitcast.10, f32[8,512]{1,0:T(8,128)} %get-tuple-element.12.refs_3_.sq0_ref, bf16[768,2048]{1,0:T(8,128)(2,1)} %refs_4_.3, ...), custom_call_target="tpu_custom_call" | custom-call | flops 99999997952 | bytes 62914560 | tf_op jit(solution)/shard_map/second/pallas_call | solution.py:876
  218.4 16.8 %renew.1 = (f32[6144,512]{1,0:T(8,128)}, bf16[768,2048]{1,0:T(8,128)(2,1)}) custom-call(f32[8,512]{1,0:T(8,128)} %get-tuple-element.12.refs_3_.sq0_ref, f32[8,512]{1,0:T(8,128)} %get-tuple-element.17.sq1_ref, f32[6144,512]{1,0:T(8,128)} %bitcast.5, bf16[6144,512]{1,0:T(8,128)(2,1)} %bitcast.6, bf16[6144,512]{1,0:T(8,128)(2,1)} %bitcast.7, ...), custom_call_target="tpu_custom_call" | custom-call | flops 12582912 | bytes 50331648 | tf_op jit(solution)/shard_map/renew/pallas_call | solution.py:912

commit v2 on v1

--- a/solution.py
+++ b/solution.py
@@ -20,7 +20,7 @@
 
 
 SHARES = ((8, 4, 4), (8, 4, 4))
-STEPS = ((1, 2, 2), (1, 2, 2))
+STEPS = ((2, 2, 2), (2, 2, 2))
 CHUNK = 256
 
 
@@ -335,7 +335,7 @@
 BLOCK = 256
 RENEW_STEPS = 4
 HALO_PIECES = 8
-HALO_LEAD = 4
+HALO_LEAD = 10
 NEAR_AT = 19
 NEAR_EVERY = 2
 
@@ -408,17 +408,16 @@
 
     if second:
         edge_ref, win_ref, rate_ref, sq_in, keys, values, queries, targets, weights = take(9)
-        g_in, attn, k_far, v_far = take(4)
+        g_in, attn = take(2)
         sums, sq_ref, mixed = take(3)
     else:
         edge_ref, win_ref, rate_ref, keys, values, queries, targets, weights = take(8)
-        sums, sq_ref, attn, k_far, v_far = take(5)
+        sums, sq_ref, attn = take(3)
     kbuf, qbuf, tbuf, wbuf, wb, g, res, acc, got, dbuf, stage, sq_all = take(12)
     send, recv, sq_send, sq_recv, load, wload, out_sem, stage_sem = take(8)
+    vbuf, halo_send, halo_recv = take(3)
     if second:
-        vbuf, gbuf, mstage, in_sem, far_sem = take(5)
-    else:
-        vbuf, halo_send, halo_recv, far_sem = take(4)
+        gbuf, mstage, in_sem, own_sem = take(4)
     pad = WIN
     assert not refs
 
@@ -445,14 +444,11 @@
     plain = (blocks - halo_blocks) * heads
     here = heads - heads // 2
 
-    def far_copies(h):
-        k = h - here
-        pairs = [(kbuf.at[h, pl.ds(0, WIN)], k_far.at[k]), (vbuf.at[k if second else h, pl.ds(0, WIN)], v_far.at[k])]
-        if second:
-            pairs = [(b, a) for a, b in pairs]
-            rows = pl.ds(0, WIN)
-            pairs.append((columns(values, h, rows), vbuf.at[k, pl.ds(WIN, WIN)]))
-        return [pltpu.make_async_copy(a, b, far_sem.at[i, k]) for i, (a, b) in enumerate(pairs)]
+    low, away = (here, heads - here) if second else (0, here)
+
+    def own_values(h):
+        k = h - low
+        return pltpu.make_async_copy(columns(values, h, pl.ds(0, WIN)), vbuf.at[k, pl.ds(WIN, WIN)], own_sem.at[k])
 
     def attention(q, v_all, h, start):
         span = WIN + BLOCK
@@ -507,8 +503,7 @@
     if second:
         attn_in(0).start()
         for h in range(here, heads):
-            for c in far_copies(h):
-                c.start()
+            own_values(h).start()
     sq_all[mine] = jnp.zeros(sq_all.shape[1:], jnp.float32)
 
     @pl.when(gives & jnp.logical_not(works))
@@ -517,27 +512,27 @@
         def _(n):
             g[n] = jnp.zeros(g.shape[1:], g.dtype)
 
-    if not second:
+    if away:
 
         @pl.when(me == 0)
         def _():
-            @pl.loop(0, heads)
-            def _(h):
-                kbuf[h, pl.ds(0, WIN)] = jnp.zeros((WIN, hd), kbuf.dtype)
-                vbuf[h, pl.ds(0, WIN)] = jnp.zeros((WIN, hd), vbuf.dtype)
+            @pl.loop(0, away)
+            def _(k):
+                kbuf[low + k, pl.ds(0, WIN)] = jnp.zeros((WIN, hd), kbuf.dtype)
+                vbuf[k, pl.ds(0, WIN)] = jnp.zeros((WIN, hd), vbuf.dtype)
 
     greet(near_size, far_size)
 
     def halo(h, first=0, size=WIN):
         rows = pl.ds(pl.multiple_of(local - WIN + first, 16), size)
         out = []
-        for i, (src, dst) in enumerate(((keys, kbuf), (values, vbuf))):
+        for i, (src, dst) in enumerate(((keys, kbuf.at[h]), (values, vbuf.at[h - low]))):
             out.append(
                 pltpu.make_async_remote_copy(
                     src_ref=columns(src, h, rows),
-                    dst_ref=dst.at[h, pl.ds(first, size)],
+                    dst_ref=dst.at[pl.ds(first, size)],
                     send_sem=halo_send.at[i],
-                    recv_sem=halo_recv.at[i, h],
+                    recv_sem=halo_recv.at[i, h - low],
                     device_id={"seq": me + 1},
                     device_id_type=pl.DeviceIdType.MESH,
                 )
@@ -670,8 +665,12 @@
 
             @pl.when((block == halo_blocks - 1) & (h >= here))
             def _():
-                for c in far_copies(h):
-                    c.wait()
+                own_values(h).wait()
+
+            @pl.when((block == halo_blocks - 1) & (h >= here) & (me > 0))
+            def _():
+                for c in halo(h):
+                    c.wait_recv()
 
             @pl.when((block < halo_blocks) & (h >= here))
             def _():
@@ -720,12 +719,12 @@
     def send_halo(i):
         size = WIN // HALO_PIECES
 
-        @pl.when((i < heads * HALO_PIECES) & (me < count - 1))
-        def _():
-            for c in halo(i // HALO_PIECES, pl.multiple_of((i % HALO_PIECES) * size, size), size):
+        @pl.when((i < away * HALO_PIECES) & (me < count - 1))
+        def _():
+            for c in halo(low + i // HALO_PIECES, pl.multiple_of((i % HALO_PIECES) * size, size), size):
                 c.start()
 
-    if not second:
+    if away:
 
         @pl.loop(0, HALO_LEAD)
         def _(i):
@@ -747,8 +746,12 @@
 
     @pl.loop(0, max(netw.length, *steps))
     def _(i):
-        if not second:
-            send_halo(i + HALO_LEAD)
+        if away:
+
+            @pl.when(i % 2 == 0)
+            def _():
+                send_halo(i // 2 + HALO_LEAD)
+
 
         @pl.when(works)
         def _():
@@ -777,24 +780,12 @@
 
     netw.drain()
     share_squares(sq_all, sq_ref, sq_send, sq_recv)
-    if not second:
-        for h in range(here, heads):
-
-            @pl.when(me > 0)
-            def _():
-                for c in halo(h):
-                    c.wait_recv()
-
-            for c in far_copies(h):
-                c.start()
-        for h in range(here, heads):
-            for c in far_copies(h):
-                c.wait()
+    if away:
 
         @pl.when(me < count - 1)
         def _():
-            for i, buf in enumerate((kbuf, vbuf)):
-                every = buf.at[pl.ds(0, heads), pl.ds(0, WIN)]
+            for i in range(2):
+                every = kbuf.at[pl.ds(low, away), pl.ds(0, WIN)]
                 pltpu.make_async_remote_copy(
                     src_ref=every, dst_ref=every, send_sem=halo_send.at[i], recv_sem=halo_recv.at[i, 0],
                     device_id={"seq": me + 1}, device_id_type=pl.DeviceIdType.MESH,
@@ -828,8 +819,7 @@
     dma = pltpu.SemaphoreType.DMA
     bf16, f32 = jnp.bfloat16, jnp.float32
     pad = WIN
-    away = heads // 2
-    far_shape = (max(away, 1), WIN, hd)
+    away = max(heads // 2, 1)
     scratch = [
         pltpu.VMEM((heads, pad + local, hd), bf16),
         pltpu.VMEM((heads, local, hd), bf16),
@@ -852,37 +842,32 @@
         dma((1,)),
         dma((2,)),
     ]
+    scratch += [
+        pltpu.VMEM((away, 2 * WIN, hd) if second else (heads, pad + local, hd), bf16),
+        dma((2,)),
+        dma((2, heads)),
+    ]
     if second:
         scratch += [
-            pltpu.VMEM((max(away, 1), 2 * WIN, hd), bf16),
             pltpu.VMEM((3 * hd // CHUNK, CHUNK, hid), bf16),
             pltpu.VMEM((2, BLOCK, hd), bf16),
             dma((2,)),
-            dma((3, max(away, 1))),
+            dma((away,)),
         ]
-        in_specs = [smem, smem, vmem, vmem] + [hbm] * 9
-        more = ()
+        in_specs = [smem, smem, vmem, vmem] + [hbm] * 7
         wide = jax.ShapeDtypeStruct(keys.shape, bf16)
     else:
-        scratch += [
-            pltpu.VMEM((heads, pad + local, hd), bf16),
-            dma((2,)),
-            dma((2, heads)),
-            dma((2, max(away, 1))),
-        ]
-        more = (jax.ShapeDtypeStruct(far_shape, bf16),) * 2
         in_specs = [smem, smem, vmem, hbm, hbm, hbm, hbm, hbm]
         wide = jax.ShapeDtypeStruct(keys.shape, f32)
     return pl.pallas_call(
         functools.partial(block_kernel, second, near, far, total_count),
         in_specs=in_specs,
-        out_specs=(hbm, vmem, hbm) + (hbm,) * len(more),
+        out_specs=(hbm, vmem, hbm),
         out_shape=(
             jax.ShapeDtypeStruct((chunks, CHUNK, hid), bf16),
             jax.ShapeDtypeStruct((8, hid), f32),
             wide,
-        )
-        + more,
+        ),
         scratch_shapes=scratch,
         compiler_params=pltpu.CompilerParams(
             collective_id=int(second), has_side_effects=True, vmem_limit_bytes=67043328
@@ -927,12 +912,12 @@
 
 def per_device(queries, keys, values, targets, token_rate, window, split, fast_init):
     total_count = float(fast_init.size * lax.axis_size("head"))
-    g0, sq0, attn, k_far, v_far = block_step(
+    g0, sq0, attn = block_step(
         False, (split, window, token_rate.T, keys, values, queries, targets, fast_init), total_count
     )
     g1, sq1, mixed = block_step(
         True,
-        (split, window, token_rate.T, sq0, keys, values, queries, targets, fast_init, g0, attn, k_far, v_far),
+        (split, window, token_rate.T, sq0, keys, values, queries, targets, fast_init, g0, attn),
         total_count,
     )
     return renew(total_count, sq0, sq1, fast_init, g0, g1, mixed)

time: 235 us -> 229 us (0.974)
  Pallas kernels: 234 us -> 227 us
    pallas_call x2, Pallas kernels: 217 us -> 210 us  [block_step(): pl.pallas_call(functools.partial(block_kernel, second, near, far, total_c...]
where the time goes in v2:
time: 229 us
  Pallas kernels  227 us (99%)
    pallas_call x2, Pallas kernels, block_step(): pl.pallas_call(functools.partial(block_kernel, second, near, far, total_c...  210 us
    pallas_call x1, Pallas kernels, renew(): pl.pallas_call(functools.partial(renew_kernel, total_count), grid=(steps,...  16.8 us

profile of v2, /device:TPU:0, one launch (start us, length us, event | category | flops | bytes accessed | tf_op | source)
XLA Modules:
  0.0 228.6 jit_solution(9440180500702341163)
XLA Ops:
  1.3 108.9 %first.1 = (bf16[24,256,512]{2,1,0:T(8,128)(2,1)}, f32[8,512]{1,0:T(8,128)}, f32[768,2048]{1,0:T(8,128)}) custom-call(s32[1]{0:T(128)S(6)} %copy.10.refs_0_, s32[4]{0:T(128)} %refs_1_.3, f32[4,768]{1,0:T(4,128)} %bitcast.9, bf16[768,2048]{1,0:T(8,128)(2,1)} %refs_4_.3, bf16[768,2048]{1,0:T(8,128)(2,1)} %refs_5_.3, bf16[768,2048]{1,0:T(8,128)(2,1)} %refs_6_.3, ...), custom_call_target="tpu_custom_call" | custom-call | flops 99999997952 | bytes 62914560 | tf_op jit(solution)/shard_map/first/pallas_call | solution.py:862
  110.2 101.6 %second.1 = (bf16[24,256,512]{2,1,0:T(8,128)(2,1)}, f32[8,512]{1,0:T(8,128)}, bf16[768,2048]{1,0:T(8,128)(2,1)}) custom-call(s32[1]{0:T(128)S(6)} %copy.10.refs_0_, s32[4]{0:T(128)} %refs_1_.3, f32[4,768]{1,0:T(4,128)} %bitcast.10, f32[8,512]{1,0:T(8,128)} %get-tuple-element.10.refs_3_.sq0_ref, bf16[768,2048]{1,0:T(8,128)(2,1)} %refs_4_.3, ...), custom_call_target="tpu_custom_call" | custom-call | flops 99999997952 | bytes 62914560 | tf_op jit(solution)/shard_map/second/pallas_call | solution.py:862
  211.8 16.8 %renew.1 = (f32[6144,512]{1,0:T(8,128)}, bf16[768,2048]{1,0:T(8,128)(2,1)}) custom-call(f32[8,512]{1,0:T(8,128)} %get-tuple-element.10.refs_3_.sq0_ref, f32[8,512]{1,0:T(8,128)} %get-tuple-element.13.sq1_ref, f32[6144,512]{1,0:T(8,128)} %bitcast.5, bf16[6144,512]{1,0:T(8,128)(2,1)} %bitcast.6, bf16[6144,512]{1,0:T(8,128)(2,1)} %bitcast.7, ...), custom_call_target="tpu_custom_call" | custom-call | flops 12582912 | bytes 50331648 | tf_op jit(solution)/shard_map/renew/pallas_call | solution.py:897

commit v3 on v2

--- a/solution.py
+++ b/solution.py
@@ -409,7 +409,7 @@
     if second:
         edge_ref, win_ref, rate_ref, sq_in, keys, values, queries, targets, weights = take(9)
         g_in, attn = take(2)
-        sums, sq_ref, mixed = take(3)
+        sums, sq_ref, mixed, base = take(4)
     else:
         edge_ref, win_ref, rate_ref, keys, values, queries, targets, weights = take(8)
         sums, sq_ref, attn = take(3)
@@ -417,7 +417,7 @@
     send, recv, sq_send, sq_recv, load, wload, out_sem, stage_sem = take(8)
     vbuf, halo_send, halo_recv = take(3)
     if second:
-        gbuf, mstage, in_sem, own_sem = take(4)
+        gbuf, mstage, in_sem, own_sem, base_sem = take(5)
     pad = WIN
     assert not refs
 
@@ -497,13 +497,8 @@
 
     for c in load_weights(0):
         c.start()
-    for h in range(heads):
-        for i in (0, 1, 2) if second else (0, 1, 2, 3):
-            load_one(i, h).start()
-    if second:
-        attn_in(0).start()
-        for h in range(here, heads):
-            own_values(h).start()
+    for i in (0, 1):
+        load_one(i, 0).start()
     sq_all[mine] = jnp.zeros(sq_all.shape[1:], jnp.float32)
 
     @pl.when(gives & jnp.logical_not(works))
@@ -544,6 +539,15 @@
     def position(rows):
         return anchor + rows + lax.broadcasted_iota(jnp.int32, (BLOCK, 1), 0)
 
+    def keep(h):
+        return pltpu.make_async_copy(wbuf, base.at[h], base_sem.at[0])
+
+    def load_next(h):
+        @pl.when(h + 1 < heads)
+        def _():
+            for c in load_weights(h + 1):
+                c.start()
+
     def prepare(h):
         for c in load_weights(h):
             c.wait()
@@ -555,12 +559,13 @@
                 w = wbuf[j, rows]
                 if second:
                     w = w - coef * gbuf[j * pieces + p].astype(jnp.float32)
+                    wbuf[j, rows] = w
                 wb[h, j, rows] = w.astype(jnp.bfloat16)
 
-        @pl.when(h + 1 < heads)
-        def _():
-            for c in load_weights(h + 1):
-                c.start()
+        if second:
+            keep(h).start()
+        else:
+            load_next(h)
 
     def backward(h, kind):
         @pl.when(kind == 0)
@@ -700,7 +705,7 @@
         h = i // per
         kind = i % per
 
-        @pl.when(h < heads)
+        @pl.when((h < heads) & works)
         def _():
             @pl.when(kind < ahead)
             def _():
@@ -712,7 +717,14 @@
                 def _():
                     outer(h, j)
 
-        @pl.when((h < heads - 1) & (kind == per - 1))
+        if second:
+
+            @pl.when((h < heads) & (kind == 1))
+            def _():
+                keep(h).wait()
+                load_next(h)
+
+        @pl.when((h < heads - 1) & (kind == per - 1) & prepares)
         def _():
             prepare(h + 1)
 
@@ -730,13 +742,24 @@
         def _(i):
             send_halo(i)
 
-    @pl.when(works)
+    prepares = (me >= 0) if second else works
+
+    @pl.when(prepares)
     def _():
         prepare(0)
 
-        @pl.loop(0, ahead)
-        def _(i):
-            gradient(i)
+    for h in range(heads):
+        for i in (0, 1, 2) if second else (0, 1, 2, 3):
+            if h > 0 or i > 1:
+                load_one(i, h).start()
+    if second:
+        attn_in(0).start()
+        for h in range(here, heads):
+            own_values(h).start()
+
+    @pl.loop(0, ahead)
+    def _(i):
+        gradient(i)
 
     if second:
         steps = [begin + units]
@@ -753,9 +776,7 @@
                 send_halo(i // 2 + HALO_LEAD)
 
 
-        @pl.when(works)
-        def _():
-            gradient(i + ahead)
+        gradient(i + ahead)
 
         netw.advance(i, finish)
         u = i - begin
@@ -778,8 +799,8 @@
             def _():
                 attend(halo_blocks - 1 - w % halo_blocks, w // halo_blocks, plain + w)
 
+    share_squares(sq_all, sq_ref, sq_send, sq_recv)
     netw.drain()
-    share_squares(sq_all, sq_ref, sq_send, sq_recv)
     if away:
 
         @pl.when(me < count - 1)
@@ -791,10 +812,12 @@
                     device_id={"seq": me + 1}, device_id_type=pl.DeviceIdType.MESH,
                 ).wait_send()
 
-    @pl.when(jnp.logical_not(works))
-    def _():
-        for c in load_weights(0):
-            c.wait()
+    if not second:
+
+        @pl.when(jnp.logical_not(works))
+        def _():
+            for c in load_weights(0):
+                c.wait()
 
     for slot in range(2):
         block_out(0, 0, slot).wait()
@@ -814,6 +837,7 @@
     smem = pl.BlockSpec(memory_space=pltpu.SMEM)
     hbm = pl.BlockSpec(memory_space=pl.ANY)
     half = CHUNK // CORES
+    more = (jax.ShapeDtypeStruct(weights.shape, jnp.float32),) if second else ()
     kinds = link_kinds(near)
     ranks = lax.axis_size("head")
     dma = pltpu.SemaphoreType.DMA
@@ -853,6 +877,7 @@
             pltpu.VMEM((2, BLOCK, hd), bf16),
             dma((2,)),
             dma((away,)),
+            dma((1,)),
         ]
         in_specs = [smem, smem, vmem, vmem] + [hbm] * 7
         wide = jax.ShapeDtypeStruct(keys.shape, bf16)
@@ -862,12 +887,13 @@
     return pl.pallas_call(
         functools.partial(block_kernel, second, near, far, total_count),
         in_specs=in_specs,
-        out_specs=(hbm, vmem, hbm),
+        out_specs=(hbm, vmem, hbm) + (hbm,) * len(more),
         out_shape=(
             jax.ShapeDtypeStruct((chunks, CHUNK, hid), bf16),
             jax.ShapeDtypeStruct((8, hid), f32),
             wide,
-        ),
+        )
+        + more,
         scratch_shapes=scratch,
         compiler_params=pltpu.CompilerParams(
             collective_id=int(second), has_side_effects=True, vmem_limit_bytes=67043328
@@ -877,27 +903,23 @@
     )(*arrays)
 
 
-def renew_kernel(total_count, sq0_ref, sq1_ref, w_ref, g0_ref, g1_ref, mixed_ref, out_ref, copy_ref):
-    coef = [
-        fast_rate / jnp.sqrt(jnp.sum(s[...]) / total_count + epsilon) for s in (sq0_ref, sq1_ref)
-    ]
-    out_ref[...] = (
-        w_ref[...] - coef[0] * g0_ref[...].astype(jnp.float32) - coef[1] * g1_ref[...].astype(jnp.float32)
-    )
+def renew_kernel(total_count, sq_ref, w_ref, g_ref, mixed_ref, out_ref, copy_ref):
+    coef = fast_rate / jnp.sqrt(jnp.sum(sq_ref[...]) / total_count + epsilon)
+    out_ref[...] = w_ref[...] - coef * g_ref[...].astype(jnp.float32)
     copy_ref[...] = mixed_ref[...]
 
 
-def renew(total_count, sq0, sq1, weights, g0, g1, mixed):
+def renew(total_count, sq, weights, g, mixed):
     flat = (-1, weights.shape[-1])
     w = weights.reshape(flat)
     steps = RENEW_STEPS
-    small = pl.BlockSpec(sq0.shape, lambda i: (0, 0))
+    small = pl.BlockSpec(sq.shape, lambda i: (0, 0))
     tile = pl.BlockSpec((w.shape[0] // steps, w.shape[1]), lambda i: (i, 0))
     rows = pl.BlockSpec((mixed.shape[0] // steps, mixed.shape[1]), lambda i: (i, 0))
     out, mixed = pl.pallas_call(
         functools.partial(renew_kernel, total_count),
         grid=(steps,),
-        in_specs=[small, small, tile, tile, tile, rows],
+        in_specs=[small, tile, tile, rows],
         out_specs=(tile, rows),
         out_shape=(
             jax.ShapeDtypeStruct(w.shape, jnp.float32),
@@ -906,7 +928,7 @@
         compiler_params=pltpu.CompilerParams(vmem_limit_bytes=67043328),
         cost_estimate=pl.CostEstimate(flops=4 * w.size, bytes_accessed=16 * w.size, transcendentals=0),
         name="renew",
-    )(sq0, sq1, w, g0.reshape(flat), g1.reshape(flat), mixed)
+    )(sq, w, g.reshape(flat), mixed)
     return mixed, out.reshape(weights.shape)
 
 
@@ -915,12 +937,12 @@
     g0, sq0, attn = block_step(
         False, (split, window, token_rate.T, keys, values, queries, targets, fast_init), total_count
     )
-    g1, sq1, mixed = block_step(
+    g1, sq1, mixed, base = block_step(
         True,
         (split, window, token_rate.T, sq0, keys, values, queries, targets, fast_init, g0, attn),
         total_count,
     )
-    return renew(total_count, sq0, sq1, fast_init, g0, g1, mixed)
+    return renew(total_count, sq1, base, g1, mixed)
 
 
 def solution(mesh):

time: 229 us -> 225 us (0.983)
  Pallas kernels: 227 us -> 224 us
    pallas_call x1, Pallas kernels: 16.8 us -> 13.2 us  [renew(): pl.pallas_call(functools.partial(renew_kernel, total_count), grid=(steps,...]
where the time goes in v3:
time: 225 us
  Pallas kernels  224 us (100%)
    pallas_call x2, Pallas kernels, block_step(): pl.pallas_call(functools.partial(block_kernel, second, near, far, total_c...  210 us
    pallas_call x1, Pallas kernels, renew(): pl.pallas_call(functools.partial(renew_kernel, total_count), grid=(steps,...  13.2 us

profile of v3, /device:TPU:0, one launch (start us, length us, event | category | flops | bytes accessed | tf_op | source)
XLA Modules:
  0.0 225.0 jit_solution(5809823705998268541)
XLA Ops:
  1.3 108.3 %first.1 = (bf16[24,256,512]{2,1,0:T(8,128)(2,1)}, f32[8,512]{1,0:T(8,128)}, f32[768,2048]{1,0:T(8,128)}) custom-call(s32[1]{0:T(128)S(6)} %copy.10.refs_0_, s32[4]{0:T(128)} %refs_1_.3, f32[4,768]{1,0:T(4,128)} %bitcast.7, bf16[768,2048]{1,0:T(8,128)(2,1)} %refs_4_.3, bf16[768,2048]{1,0:T(8,128)(2,1)} %refs_5_.3, bf16[768,2048]{1,0:T(8,128)(2,1)} %refs_6_.3, ...), custom_call_target="tpu_custom_call" | custom-call | flops 99999997952 | bytes 62914560 | tf_op jit(solution)/shard_map/first/pallas_call | solution.py:887
  109.6 102.2 %second.1 = (bf16[24,256,512]{2,1,0:T(8,128)(2,1)}, f32[8,512]{1,0:T(8,128)}, bf16[768,2048]{1,0:T(8,128)(2,1)}, f32[4,3,512,512]{3,2,1,0:T(8,128)}) custom-call(s32[1]{0:T(128)S(6)} %copy.10.refs_0_, s32[4]{0:T(128)} %refs_1_.3, f32[4,768]{1,0:T(4,128)} %bitcast.8, f32[8,512]{1,0:T(8,128)} %get-tuple-element.11.refs_3_, bf16[768,2048]{1,0:T(8,128)(2,1)} %refs_4_.3, ...), custom_call_target="tpu_custom_call" | custom-call | flops 99999997952 | bytes 62914560 | tf_op jit(solution)/shard_map/second/pallas_call | solution.py:887
  211.8 13.2 %renew.1 = (f32[6144,512]{1,0:T(8,128)}, bf16[768,2048]{1,0:T(8,128)(2,1)}) custom-call(f32[8,512]{1,0:T(8,128)} %get-tuple-element.14.sq_ref, f32[6144,512]{1,0:T(8,128)} %bitcast.4, bf16[6144,512]{1,0:T(8,128)(2,1)} %bitcast.5, bf16[768,2048]{1,0:T(8,128)(2,1)} %get-tuple-element.17.mixed_ref), custom_call_target="tpu_custom_call" | custom-call | flops 12582912 | bytes 50331648 | tf_op jit(solution)/shard_map/renew/pallas_call | solution.py:919

commit v4 on v3

--- a/solution.py
+++ b/solution.py
@@ -334,8 +334,8 @@
 
 BLOCK = 256
 RENEW_STEPS = 4
-HALO_PIECES = 8
-HALO_LEAD = 10
+HALO_PIECES = 16
+HALO_LEAD = 20
 NEAR_AT = 19
 NEAR_EVERY = 2
 
@@ -771,9 +771,7 @@
     def _(i):
         if away:
 
-            @pl.when(i % 2 == 0)
-            def _():
-                send_halo(i // 2 + HALO_LEAD)
+            send_halo(i + HALO_LEAD)
 
 
         gradient(i + ahead)

time: 225 us -> 225 us (level)
  no operation moved by 1% of the time
where the time goes in v4:
time: 225 us
  Pallas kernels  224 us (100%)
    pallas_call x2, Pallas kernels, block_step(): pl.pallas_call(functools.partial(block_kernel, second, near, far, total_c...  210 us
    pallas_call x1, Pallas kernels, renew(): pl.pallas_call(functools.partial(renew_kernel, total_count), grid=(steps,...  13.2 us

profile of v4, /device:TPU:0, one launch (start us, length us, event | category | flops | bytes accessed | tf_op | source)
XLA Modules:
  0.0 224.8 jit_solution(3640892985960958658)
XLA Ops:
  1.3 108.6 %first.1 = (bf16[24,256,512]{2,1,0:T(8,128)(2,1)}, f32[8,512]{1,0:T(8,128)}, f32[768,2048]{1,0:T(8,128)}) custom-call(s32[1]{0:T(128)S(6)} %copy.10.refs_0_, s32[4]{0:T(128)} %refs_1_.3, f32[4,768]{1,0:T(4,128)} %bitcast.7, bf16[768,2048]{1,0:T(8,128)(2,1)} %refs_4_.3, bf16[768,2048]{1,0:T(8,128)(2,1)} %refs_5_.3, bf16[768,2048]{1,0:T(8,128)(2,1)} %refs_6_.3, ...), custom_call_target="tpu_custom_call" | custom-call | flops 99999997952 | bytes 62914560 | tf_op jit(solution)/shard_map/first/pallas_call | solution.py:885
  109.9 101.7 %second.1 = (bf16[24,256,512]{2,1,0:T(8,128)(2,1)}, f32[8,512]{1,0:T(8,128)}, bf16[768,2048]{1,0:T(8,128)(2,1)}, f32[4,3,512,512]{3,2,1,0:T(8,128)}) custom-call(s32[1]{0:T(128)S(6)} %copy.10.refs_0_, s32[4]{0:T(128)} %refs_1_.3, f32[4,768]{1,0:T(4,128)} %bitcast.8, f32[8,512]{1,0:T(8,128)} %get-tuple-element.11.refs_3_, bf16[768,2048]{1,0:T(8,128)(2,1)} %refs_4_.3, ...), custom_call_target="tpu_custom_call" | custom-call | flops 99999997952 | bytes 62914560 | tf_op jit(solution)/shard_map/second/pallas_call | solution.py:885
  211.6 13.2 %renew.1 = (f32[6144,512]{1,0:T(8,128)}, bf16[768,2048]{1,0:T(8,128)(2,1)}) custom-call(f32[8,512]{1,0:T(8,128)} %get-tuple-element.14.sq_ref, f32[6144,512]{1,0:T(8,128)} %bitcast.4, bf16[6144,512]{1,0:T(8,128)(2,1)} %bitcast.5, bf16[768,2048]{1,0:T(8,128)(2,1)} %get-tuple-element.17.mixed_ref), custom_call_target="tpu_custom_call" | custom-call | flops 12582912 | bytes 50331648 | tf_op jit(solution)/shard_map/renew/pallas_call | solution.py:917

commit v5 on v4

--- a/solution.py
+++ b/solution.py
@@ -333,7 +333,7 @@
 
 
 BLOCK = 256
-RENEW_STEPS = 4
+RENEW_STEPS = 3
 HALO_PIECES = 16
 HALO_LEAD = 20
 NEAR_AT = 19

time: 225 us -> 227 us (level)
  no operation moved by 1% of the time
where the time goes in v5:
time: 227 us; the launch traced here: 226 us
  Pallas kernels  225 us (99%)
    pallas_call x2, Pallas kernels, block_step(): pl.pallas_call(functools.partial(block_kernel, second, near, far, total_c...  210 us
    pallas_call x1, Pallas kernels, renew(): pl.pallas_call(functools.partial(renew_kernel, total_count), grid=(steps,...  14.7 us

profile of v5, /device:TPU:0, one launch (start us, length us, event | category | flops | bytes accessed | tf_op | source)
XLA Modules:
  0.0 226.4 jit_solution(5841671900515590267)
XLA Ops:
  1.3 108.6 %first.1 = (bf16[24,256,512]{2,1,0:T(8,128)(2,1)}, f32[8,512]{1,0:T(8,128)}, f32[768,2048]{1,0:T(8,128)}) custom-call(s32[1]{0:T(128)S(6)} %copy.10.refs_0_, s32[4]{0:T(128)} %refs_1_.3, f32[4,768]{1,0:T(4,128)} %bitcast.7, bf16[768,2048]{1,0:T(8,128)(2,1)} %refs_4_.3, bf16[768,2048]{1,0:T(8,128)(2,1)} %refs_5_.3, bf16[768,2048]{1,0:T(8,128)(2,1)} %refs_6_.3, ...), custom_call_target="tpu_custom_call" | custom-call | flops 99999997952 | bytes 62914560 | tf_op jit(solution)/shard_map/first/pallas_call | solution.py:885
  109.9 101.7 %second.1 = (bf16[24,256,512]{2,1,0:T(8,128)(2,1)}, f32[8,512]{1,0:T(8,128)}, bf16[768,2048]{1,0:T(8,128)(2,1)}, f32[4,3,512,512]{3,2,1,0:T(8,128)}) custom-call(s32[1]{0:T(128)S(6)} %copy.10.refs_0_, s32[4]{0:T(128)} %refs_1_.3, f32[4,768]{1,0:T(4,128)} %bitcast.8, f32[8,512]{1,0:T(8,128)} %get-tuple-element.11.refs_3_, bf16[768,2048]{1,0:T(8,128)(2,1)} %refs_4_.3, ...), custom_call_target="tpu_custom_call" | custom-call | flops 99999997952 | bytes 62914560 | tf_op jit(solution)/shard_map/second/pallas_call | solution.py:885
  211.6 14.7 %renew.1 = (f32[6144,512]{1,0:T(8,128)}, bf16[768,2048]{1,0:T(8,128)(2,1)}) custom-call(f32[8,512]{1,0:T(8,128)} %get-tuple-element.14.sq_ref, f32[6144,512]{1,0:T(8,128)} %bitcast.4, bf16[6144,512]{1,0:T(8,128)(2,1)} %bitcast.5, bf16[768,2048]{1,0:T(8,128)(2,1)} %get-tuple-element.17.mixed_ref), custom_call_target="tpu_custom_call" | custom-call | flops 12582912 | bytes 50331648 | tf_op jit(solution)/shard_map/renew/pallas_call | solution.py:917
